TPU v7x, 32 devices: a whole 2x2x4 slice. The times are simulated.
32 devices in a mesh: dp: 2 (over x), ctx: 4 (over y, core), tp: 4 (over z).
Axes of the slice: x: 2, y: 2, z: 4, core: 2. Of those that a mesh axis runs over, the one named last changes fastest.
Arguments:
- hidden_in: bfloat16 [2, 8192, 1024], P('dp', ('ctx', 'tp')), may hold values from -6 to 6
- attn_gain: bfloat16 [1024], replicated, may hold values from 0.5 to 1.5
- qkv_weight: bfloat16 [1024, 3, 1024], P(None, None, 'tp'), may hold values from -0.1875 to 0.1875
- out_weight: bfloat16 [1024, 1024], P('tp'), may hold values from -1.5 to 1.5
- mlp_gain: bfloat16 [1024], replicated, may hold values from 0.5 to 1.5
- wide_weight: bfloat16 [1024, 2, 2624], P(None, None, 'tp'), may hold values from -0.1875 to 0.1875
- down_weight: bfloat16 [2624, 1024], P('tp'), may hold values from -0.125 to 0.125
- lengths: int32 [2, 16], P('dp'), may hold values from 1 to 5120, 7680 in all within a row
- cotangent: bfloat16 [2, 8192, 1024], P('dp', ('ctx', 'tp')), may hold values from -6 to 6
Outputs:
- result: bfloat16 [2, 8192, 1024], P('dp', ('ctx', 'tp'))
- input_grad: float32 [2, 8192, 1024], P('dp', ('ctx', 'tp'))
- qkv_weight_grad: float32 [1024, 3, 1024], P(('dp', 'ctx'), None, 'tp')
- out_weight_grad: float32 [1024, 1024], P('tp', ('dp', 'ctx'))
- wide_weight_grad: float32 [1024, 2, 2624], P(('dp', 'ctx'), None, 'tp')
- down_weight_grad: float32 [2624, 1024], P('tp', ('dp', 'ctx'))
- attn_gain_grad: float32 [1024], replicated
- mlp_gain_grad: float32 [1024], replicated
Inputs may be any that keep to these rules, and one draw needn't show every extreme that they name: Each row's 16 lengths sum to exactly 7680, the rest of the row being padding, and the longest is exactly 5120.
All inputs are finite; a program needn't handle non-finite values.
Results may differ from a plain program's by a relative error of at most 0.02.
Values may be sent and summed in bfloat16 or wider, within the bound.
A program may use at most 384 MiB of HBM per device.

v0:
```python
from functools import partial
import math

import jax
import jax.numpy as jnp
from jax import lax
from jax.sharding import PartitionSpec as P

HD = 64


eps_norm = 1e-05
theta_base = 160000.0
neg_fill = -1e30
block_rows = 512


def layout(length_row, row_length):
    doc_count = length_row.shape[0]
    doc_ends = jnp.cumsum(length_row)
    starts = doc_ends - length_row
    places = lax.iota(jnp.int32, row_length)
    segment = jnp.sum((places[:, None] >= doc_ends[None, :]).astype(jnp.int32), axis=1)
    owned = segment[:, None] == lax.iota(jnp.int32, doc_count)[None, :]
    offset = jnp.sum(jnp.where(owned, starts[None, :], 0), axis=1)
    filled_to = doc_ends[doc_count - 1]
    offset = jnp.where(segment == doc_count, filled_to, offset)
    return (segment, places - offset, places < filled_to)


def normalize(row_values, norm_gain):
    row_mean = jnp.mean(row_values, axis=-1, keepdims=True)
    centered = row_values - row_mean
    variance = jnp.mean(centered * centered, axis=-1, keepdims=True)
    return centered * lax.rsqrt(variance + eps_norm) * norm_gain


def rotate(field_in, in_doc, head_count):
    half_size = HD // 2
    frequency = jnp.exp(lax.iota(jnp.float32, half_size) * (-2.0 * math.log(theta_base) / HD))
    angles = in_doc.astype(jnp.float32)[..., None] * frequency
    cosine = jnp.cos(angles)[..., None, :]
    sine_part = jnp.sin(angles)[..., None, :]
    shaped = field_in.reshape(field_in.shape[:-1] + (head_count, HD))
    first_half = shaped[..., :half_size]
    second = shaped[..., half_size:]
    turned = jnp.concatenate(
        [first_half * cosine - second * sine_part, second * cosine + first_half * sine_part],
        axis=-1,
    )
    return turned.reshape(field_in.shape)


def rotate_pair(first_in, second_in, in_doc, head_count):
    return (rotate(first_in, in_doc, head_count), rotate(second_in, in_doc, head_count))


def geglu(gate_in, up_in):
    return jax.nn.gelu(gate_in, approximate=False) * up_in


def recompute(query_block, seg_block, key_part, seg_keys, log_block, score_scale):
    scores = (
        jnp.einsum("qhd,khd->hqk", query_block, key_part, preferred_element_type=jnp.float32)
        * score_scale
    )
    masked = jnp.where((seg_block[:, None] == seg_keys[None, :])[None], scores, neg_fill)
    return jnp.exp(masked - jnp.transpose(log_block)[:, :, None])


def body(
    hidden_in,
    attn_gain,
    qkv_weight,
    out_weight,
    mlp_gain,
    wide_weight,
    down_weight,
    lengths,
    cotangent,
):
    share = hidden_in.shape[1]
    group = share * lax.axis_size("tp")
    row_length = group * lax.axis_size("ctx")
    segment, in_doc, filled = layout(lengths[0], row_length)
    group_start = lax.axis_index("ctx") * group
    share_start = group_start + lax.axis_index("tp") * share
    seg_group = lax.dynamic_slice_in_dim(segment, group_start, group)
    doc_group = lax.dynamic_slice_in_dim(in_doc, group_start, group)
    live_share = lax.dynamic_slice_in_dim(filled, share_start, share)[:, None]
    head_count = qkv_weight.shape[2] // HD
    score_scale = 1.0 / math.sqrt(HD)
    step_rows = min(block_rows, group)
    block_count = group // step_rows
    inputs = hidden_in[0].astype(jnp.float32)
    normed_one, norm_back_one = jax.vjp(normalize, inputs, attn_gain.astype(jnp.float32))
    normed_full = lax.all_gather(normed_one.astype(jnp.bfloat16), "tp", axis=0, tiled=True)
    mixed_cols = jnp.einsum(
        "td,dcf->tcf", normed_full, qkv_weight, preferred_element_type=jnp.float32
    )
    turned, turn_back = jax.vjp(
        partial(rotate_pair, in_doc=doc_group, head_count=head_count),
        mixed_cols[:, 0],
        mixed_cols[:, 1],
    )
    queries = turned[0].astype(jnp.bfloat16)
    key_rows = turned[1].astype(jnp.bfloat16)
    value_rows = mixed_cols[:, 2].astype(jnp.bfloat16)
    keys_all, values_all = (
        lax.all_gather(key_rows, "ctx", axis=0, tiled=True),
        lax.all_gather(value_rows, "ctx", axis=0, tiled=True),
    )
    key_heads = keys_all.reshape(row_length, head_count, HD)
    value_heads = values_all.reshape(row_length, head_count, HD)

    def forward_block(packed):
        query_block, seg_block = packed
        scores = (
            jnp.einsum("qhd,khd->hqk", query_block, key_heads, preferred_element_type=jnp.float32)
            * score_scale
        )
        masked = jnp.where((seg_block[:, None] == segment[None, :])[None], scores, neg_fill)
        row_peak = jnp.max(masked, axis=-1, keepdims=True)
        log_total = row_peak + jnp.log(jnp.sum(jnp.exp(masked - row_peak), axis=-1, keepdims=True))
        weights = jnp.exp(masked - log_total).astype(jnp.bfloat16)
        outputs = jnp.einsum(
            "hqk,khd->qhd", weights, value_heads, preferred_element_type=jnp.float32
        )
        return (outputs.reshape(step_rows, head_count * HD), jnp.transpose(log_total[:, :, 0]))

    query_blocks = queries.reshape(block_count, step_rows, head_count, HD)
    seg_blocks = seg_group.reshape(block_count, step_rows)
    attended, log_totals = lax.map(forward_block, (query_blocks, seg_blocks))
    attended = attended.reshape(group, head_count * HD).astype(jnp.bfloat16)
    log_totals = log_totals.reshape(group, head_count)
    middle = inputs + lax.psum_scatter(
        jnp.dot(attended, out_weight, preferred_element_type=jnp.float32),
        "tp",
        scatter_dimension=0,
        tiled=True,
    )
    normed_two, norm_back_two = jax.vjp(normalize, middle, mlp_gain.astype(jnp.float32))
    normed_two_full = lax.all_gather(normed_two.astype(jnp.bfloat16), "tp", axis=0, tiled=True)
    wide_cols = jnp.einsum(
        "td,dcf->tcf", normed_two_full, wide_weight, preferred_element_type=jnp.float32
    )
    product, geglu_back = jax.vjp(geglu, wide_cols[:, 0], wide_cols[:, 1])
    product = product.astype(jnp.bfloat16)
    mlp_share = lax.psum_scatter(
        jnp.dot(product, down_weight, preferred_element_type=jnp.float32).astype(jnp.bfloat16),
        "tp",
        scatter_dimension=0,
        tiled=True,
    ).astype(jnp.float32)
    result = jnp.where(live_share, middle + mlp_share, 0.0).astype(jnp.bfloat16)
    grad_share = jnp.where(live_share, cotangent[0], jnp.zeros_like(cotangent[0]))
    grad_full = lax.all_gather(grad_share, "tp", axis=0, tiled=True)
    down_grad = jnp.einsum("tf,td->fd", product, grad_full, preferred_element_type=jnp.float32)
    d_product = jnp.einsum("td,fd->tf", grad_full, down_weight, preferred_element_type=jnp.float32)
    d_gate, d_up = geglu_back(d_product)
    d_wide = jnp.stack([d_gate, d_up], axis=1).astype(jnp.bfloat16)
    wide_grad = jnp.einsum(
        "td,tcf->dcf", normed_two_full, d_wide, preferred_element_type=jnp.float32
    )
    d_normed_two = lax.psum_scatter(
        jnp.einsum("tcf,dcf->td", d_wide, wide_weight, preferred_element_type=jnp.float32).astype(
            jnp.bfloat16
        ),
        "tp",
        scatter_dimension=0,
        tiled=True,
    ).astype(jnp.float32)
    d_middle_norm, gain_two_grad = norm_back_two(d_normed_two)
    d_middle = grad_share.astype(jnp.float32) + d_middle_norm
    branch_full = lax.all_gather(d_middle.astype(jnp.bfloat16), "tp", axis=0, tiled=True)
    out_grad = jnp.einsum("tf,td->fd", attended, branch_full, preferred_element_type=jnp.float32)
    d_attended = jnp.einsum(
        "td,fd->tf", branch_full, out_weight, preferred_element_type=jnp.float32
    ).astype(jnp.bfloat16)
    grad_blocks = d_attended.reshape(block_count, step_rows, head_count, HD)
    log_blocks = log_totals.reshape(block_count, step_rows, head_count)

    def query_side(carry, packed):
        query_block, grad_block, seg_block, log_block = packed
        probs = recompute(query_block, seg_block, key_heads, segment, log_block, score_scale)
        d_probs = jnp.einsum(
            "qhd,khd->hqk", grad_block, value_heads, preferred_element_type=jnp.float32
        )
        row_delta = jnp.sum(probs * d_probs, axis=-1)
        d_scores = (probs * (d_probs - row_delta[:, :, None])).astype(jnp.bfloat16)
        d_query = (
            jnp.einsum("hqk,khd->qhd", d_scores, key_heads, preferred_element_type=jnp.float32)
            * score_scale
        )
        key_acc, value_acc = carry
        key_acc = (
            key_acc
            + jnp.einsum("hqk,qhd->khd", d_scores, query_block, preferred_element_type=jnp.float32)
            * score_scale
        )
        value_acc = value_acc + jnp.einsum(
            "hqk,qhd->khd",
            probs.astype(jnp.bfloat16),
            grad_block,
            preferred_element_type=jnp.float32,
        )
        carry = (key_acc, value_acc)
        return (carry, (d_query.reshape(step_rows, head_count * HD), jnp.transpose(row_delta)))

    zero_rows = jnp.zeros((row_length, head_count, HD), jnp.float32)
    start_carry = (zero_rows, zero_rows)
    carry_out, (d_query_blocks, delta_blocks) = lax.scan(
        query_side, start_carry, (query_blocks, grad_blocks, seg_blocks, log_blocks)
    )
    d_query = d_query_blocks.reshape(group, head_count * HD)
    key_grad_all = carry_out[0].reshape(row_length, head_count * HD)
    value_grad_all = carry_out[1].reshape(row_length, head_count * HD)
    d_key, d_value = (
        lax.psum_scatter(
            key_grad_all.astype(jnp.bfloat16), "ctx", scatter_dimension=0, tiled=True
        ).astype(jnp.float32),
        lax.psum_scatter(
            value_grad_all.astype(jnp.bfloat16), "ctx", scatter_dimension=0, tiled=True
        ).astype(jnp.float32),
    )
    d_query_raw, d_key_raw = turn_back((d_query, d_key))
    d_mixed = jnp.stack([d_query_raw, d_key_raw, d_value], axis=1).astype(jnp.bfloat16)
    qkv_grad = jnp.einsum("td,tcf->dcf", normed_full, d_mixed, preferred_element_type=jnp.float32)
    d_normed_one = lax.psum_scatter(
        jnp.einsum("tcf,dcf->td", d_mixed, qkv_weight, preferred_element_type=jnp.float32).astype(
            jnp.bfloat16
        ),
        "tp",
        scatter_dimension=0,
        tiled=True,
    ).astype(jnp.float32)
    d_input_norm, gain_one_grad = norm_back_one(d_normed_one)
    input_grad = d_middle + d_input_norm
    qkv_part, out_part, wide_part, down_part = (
        lax.psum_scatter(
            qkv_grad.astype(jnp.bfloat16), ("dp", "ctx"), scatter_dimension=0, tiled=True
        ).astype(jnp.float32),
        lax.psum_scatter(
            out_grad.astype(jnp.bfloat16), ("dp", "ctx"), scatter_dimension=1, tiled=True
        ).astype(jnp.float32),
        lax.psum_scatter(
            wide_grad.astype(jnp.bfloat16), ("dp", "ctx"), scatter_dimension=0, tiled=True
        ).astype(jnp.float32),
        lax.psum_scatter(
            down_grad.astype(jnp.bfloat16), ("dp", "ctx"), scatter_dimension=1, tiled=True
        ).astype(jnp.float32),
    )
    gain_one_sum, gain_two_sum = lax.psum((gain_one_grad, gain_two_grad), ("dp", "ctx", "tp"))
    return (
        result[None],
        input_grad[None],
        qkv_part,
        out_part,
        wide_part,
        down_part,
        gain_one_sum,
        gain_two_sum,
    )


def solution(mesh):
    placed = (
        P("dp", ("ctx", "tp"), None),
        P(),
        P(None, None, "tp"),
        P("tp", None),
        P(),
        P(None, None, "tp"),
        P("tp", None),
        P("dp", None),
        P("dp", ("ctx", "tp"), None),
    )
    return jax.shard_map(
        body,
        mesh=mesh,
        in_specs=placed,
        out_specs=(
            P("dp", ("ctx", "tp"), None),
            P("dp", ("ctx", "tp"), None),
            P(("dp", "ctx"), None, "tp"),
            P("tp", ("dp", "ctx")),
            P(("dp", "ctx"), None, "tp"),
            P("tp", ("dp", "ctx")),
            P(),
            P(),
        ),
        check_vma=False,
    )
```

profile of v0, /device:TPU:0, one launch (start us, length us, event | category | flops | bytes accessed | tf_op | source)
XLA Modules:
  0.0 2395.5 jit_solution(8108458750119257213)
XLA Ops:
  17.9 80.7 %all-gather.8.cloned.1.call-done = bf16[2048,1024]{1,0:T(8,128)(2,1)} async-done(((bf16[512,1024]{1,0:T(8,128)(2,1)}), bf16[2048,1024]{1,0:T(8,128)(2,1)}) %all-gather.8.cloned.1.call-update) | async-done | bytes 4194320 | tf_op jit(solution)/shard_map/all_gather | solution.py:97
  142.9 36.7 %all-gather.18.cloned.1.call-done = bf16[8192,1,256]{0,2,1:T(8,128)(2,1)} async-done(((bf16[2048,1,256]{0,2,1:T(8,128)(2,1)}), bf16[8192,1,256]{0,2,1:T(8,128)(2,1)}) %all-gather.18.cloned.1.call-update) | async-done | bytes 4194320 | tf_op jit(solution)/shard_map/all_gather | solution.py:111
  179.6 337.9 %while.27 = (s32[]{:T(128)}, bf16[4,512,256]{2,1,0:T(8,128)(2,1)}, f32[4,512,4]{1,2,0:T(4,128)}, s32[4,512]{1,0:T(4,128)S(1)}, s32[8192]{0:T(1024)S(1)}, /*index...) while((s32[]{:T(128)}, bf16[4,512,256]{2,1,0:T(8,128)(2,1)}, ...), condition=%wide.region_8.9_spmd, body=%wide.region_5.8_spmd.sunk | while | flops 4483708928 | bytes 228169840 | solution.py:133
  526.6 141.5 %reduce-scatter.17.cloned.1.call-done = f32[512,1024]{1,0:T(8,128)} async-done(((f32[2048,1024]{1,0:T(8,128)}), f32[512,1024]{1,0:T(8,128)}) %reduce-scatter.17.cloned.1.call-update) | async-done | bytes 2097168 | tf_op jit(solution)/shard_map/reduce_scatter | solution.py:136
  672.9 78.7 %all-gather.14.cloned.1.call-done = bf16[2048,1024]{1,0:T(8,128)(2,1)} async-done(((bf16[512,1024]{1,0:T(8,128)(2,1)}), bf16[2048,1024]{1,0:T(8,128)(2,1)}) %all-gather.14.cloned.1.call-update) | async-done | bytes 4194320 | tf_op jit(solution)/shard_map/all_gather | solution.py:157
  759.5 72.8 %all-gather.12.cloned.1.call-done = bf16[2048,1024]{1,0:T(8,128)(2,1)} async-done(((bf16[512,1024]{1,0:T(8,128)(2,1)}), bf16[2048,1024]{1,0:T(8,128)(2,1)}) %all-gather.12.cloned.1.call-update) | async-done | bytes 4194320 | tf_op jit(solution)/shard_map/all_gather | solution.py:143
  875.7 67.2 %reduce-scatter.21.cloned.1.call-done = bf16[512,1024]{1,0:T(8,128)(2,1)} async-done(((bf16[2048,1024]{1,0:T(8,128)(2,1)}), bf16[512,1024]{1,0:T(8,128)(2,1)}) %reduce-scatter.21.cloned.1.call-update) | async-done | bytes 1048592 | tf_op jit(solution)/shard_map/reduce_scatter | solution.py:165
  945.6 77.1 %reduce-scatter.19.cloned.1.call-done = bf16[512,1024]{1,0:T(8,128)(2,1)} async-done(((bf16[2048,1024]{1,0:T(8,128)(2,1)}), bf16[512,1024]{1,0:T(8,128)(2,1)}) %reduce-scatter.19.cloned.1.call-update) | async-done | bytes 1048592 | tf_op jit(solution)/shard_map/reduce_scatter | solution.py:149
  1030.0 81.3 %all-gather.16.cloned.1.call-done = bf16[2048,1024]{1,0:T(8,128)(2,1)} async-done(((bf16[512,1024]{1,0:T(8,128)(2,1)}), bf16[2048,1024]{1,0:T(8,128)(2,1)}) %all-gather.16.cloned.1.call-update) | async-done | bytes 4194320 | tf_op jit(solution)/shard_map/all_gather | solution.py:175
  1119.5 874.7 %while.28 = (s32[]{:T(128)}, f32[8192,4,64]{0,2,1:T(8,128)}, f32[8192,4,64]{0,2,1:T(8,128)}, f32[4,512,256]{1,0,2:T(4,128)}, bf16[4,512,4,64]{1,3,2,0:T(8,128)(2...) while((s32[]{:T(128)}, f32[8192,4,64]{0,2,1:T(8,128)}, ...), condition=%wide.region_18.19_spmd.clone, body=%wide.region_16.18_spmd.clone.sunk | while | flops 11003885568 | bytes 570325120 | solution.py:212
  1180.4 51.8 %multiply_reduce_fusion.3 = (f32[4,512]{1,0:T(4,128)S(1)}, f32[4,512,8192]{2,1,0:T(8,128)}) fusion(f32[4,512,8192]{2,1,0:T(8,128)} %fusion.158, f32[4,512]{1,0:T(4,128)S(1)} %dynamic-slice_bitcast_fusion.2, pred[512,8192]{1,0:T(8,128)(4,1)} %broadcast_compare_fusion.5, bf16[8192,4,64]{0,2,1:T(8,128)(2,1)} %get-tuple-element.489, ...), kind=kOutput, calls=%fused_computation.18.clone.2 | convolution fusion | flops 2231367680 | bytes 142884864 | tf_op jit(solution)/shard_map/while/body/eval_jaxpr/qhd,khd->hqk/dot_general | solution.py:186
  1232.3 54.2 %multiply_convert_fusion.5 = bf16[4,512,8192]{2,1,0:T(8,128)(2,1)} fusion(f32[4,512,8192]{2,1,0:T(8,128)} %get-tuple-element.424, f32[4,512,8192]{2,1,0:T(8,128)} %fusion.158, f32[4,512]{1,0:T(4,128)S(1)} %get-tuple-element.425, f32[4,512]{1,0:T(4,128)S(1)} %dynamic-slice_bitcast_fusion.2, pred[512,8192]{1,0:T(8,128)(4,1)} %broadcast_compare_fusion.5), kind=kLoop, calls=%fused_computation.17.clone.1 | loop fusion | flops 100663296 | bytes 171982848 | tf_op jit(solution)/shard_map/while/body/eval_jaxpr/convert_element_type | solution.py:190
  1397.7 51.8 %multiply_reduce_fusion.3 = (f32[4,512]{1,0:T(4,128)S(1)}, f32[4,512,8192]{2,1,0:T(8,128)}) fusion(f32[4,512,8192]{2,1,0:T(8,128)} %fusion.158, f32[4,512]{1,0:T(4,128)S(1)} %dynamic-slice_bitcast_fusion.2, pred[512,8192]{1,0:T(8,128)(4,1)} %broadcast_compare_fusion.5, bf16[8192,4,64]{0,2,1:T(8,128)(2,1)} %get-tuple-element.489, ...), kind=kOutput, calls=%fused_computation.18.clone.2 | convolution fusion | flops 2231367680 | bytes 142884864 | tf_op jit(solution)/shard_map/while/body/eval_jaxpr/qhd,khd->hqk/dot_general | solution.py:186
  1449.5 54.2 %multiply_convert_fusion.5 = bf16[4,512,8192]{2,1,0:T(8,128)(2,1)} fusion(f32[4,512,8192]{2,1,0:T(8,128)} %get-tuple-element.424, f32[4,512,8192]{2,1,0:T(8,128)} %fusion.158, f32[4,512]{1,0:T(4,128)S(1)} %get-tuple-element.425, f32[4,512]{1,0:T(4,128)S(1)} %dynamic-slice_bitcast_fusion.2, pred[512,8192]{1,0:T(8,128)(4,1)} %broadcast_compare_fusion.5), kind=kLoop, calls=%fused_computation.17.clone.1 | loop fusion | flops 100663296 | bytes 171982848 | tf_op jit(solution)/shard_map/while/body/eval_jaxpr/convert_element_type | solution.py:190
  1617.4 51.8 %multiply_reduce_fusion.3 = (f32[4,512]{1,0:T(4,128)S(1)}, f32[4,512,8192]{2,1,0:T(8,128)}) fusion(f32[4,512,8192]{2,1,0:T(8,128)} %fusion.158, f32[4,512]{1,0:T(4,128)S(1)} %dynamic-slice_bitcast_fusion.2, pred[512,8192]{1,0:T(8,128)(4,1)} %broadcast_compare_fusion.5, bf16[8192,4,64]{0,2,1:T(8,128)(2,1)} %get-tuple-element.489, ...), kind=kOutput, calls=%fused_computation.18.clone.2 | convolution fusion | flops 2231367680 | bytes 142884864 | tf_op jit(solution)/shard_map/while/body/eval_jaxpr/qhd,khd->hqk/dot_general | solution.py:186
  1669.2 54.2 %multiply_convert_fusion.5 = bf16[4,512,8192]{2,1,0:T(8,128)(2,1)} fusion(f32[4,512,8192]{2,1,0:T(8,128)} %get-tuple-element.424, f32[4,512,8192]{2,1,0:T(8,128)} %fusion.158, f32[4,512]{1,0:T(4,128)S(1)} %get-tuple-element.425, f32[4,512]{1,0:T(4,128)S(1)} %dynamic-slice_bitcast_fusion.2, pred[512,8192]{1,0:T(8,128)(4,1)} %broadcast_compare_fusion.5), kind=kLoop, calls=%fused_computation.17.clone.1 | loop fusion | flops 100663296 | bytes 171982848 | tf_op jit(solution)/shard_map/while/body/eval_jaxpr/convert_element_type | solution.py:190
  1837.1 51.8 %multiply_reduce_fusion.3 = (f32[4,512]{1,0:T(4,128)S(1)}, f32[4,512,8192]{2,1,0:T(8,128)}) fusion(f32[4,512,8192]{2,1,0:T(8,128)} %fusion.158, f32[4,512]{1,0:T(4,128)S(1)} %dynamic-slice_bitcast_fusion.2, pred[512,8192]{1,0:T(8,128)(4,1)} %broadcast_compare_fusion.5, bf16[8192,4,64]{0,2,1:T(8,128)(2,1)} %get-tuple-element.489, ...), kind=kOutput, calls=%fused_computation.18.clone.2 | convolution fusion | flops 2231367680 | bytes 142884864 | tf_op jit(solution)/shard_map/while/body/eval_jaxpr/qhd,khd->hqk/dot_general | solution.py:186
  1888.9 54.2 %multiply_convert_fusion.5 = bf16[4,512,8192]{2,1,0:T(8,128)(2,1)} fusion(f32[4,512,8192]{2,1,0:T(8,128)} %get-tuple-element.424, f32[4,512,8192]{2,1,0:T(8,128)} %fusion.158, f32[4,512]{1,0:T(4,128)S(1)} %get-tuple-element.425, f32[4,512]{1,0:T(4,128)S(1)} %dynamic-slice_bitcast_fusion.2, pred[512,8192]{1,0:T(8,128)(4,1)} %broadcast_compare_fusion.5), kind=kLoop, calls=%fused_computation.17.clone.1 | loop fusion | flops 100663296 | bytes 171982848 | tf_op jit(solution)/shard_map/while/body/eval_jaxpr/convert_element_type | solution.py:190
  2050.0 40.7 %reduce-scatter.25.cloned.1.call-done = bf16[2048,256]{1,0:T(8,128)(2,1)} async-done(((bf16[8192,256]{1,0:T(8,128)(2,1)}), bf16[2048,256]{1,0:T(8,128)(2,1)}) %reduce-scatter.25.cloned.1.call-update) | async-done | bytes 1048592 | tf_op jit(solution)/shard_map/reduce_scatter | solution.py:222
  2134.2 46.4 %reduce-scatter.33.cloned.1.call-done = bf16[128,1312]{1,0:T(8,128)(2,1)} async-done(((bf16[1024,1312]{1,0:T(8,128)(2,1)}), bf16[128,1312]{1,0:T(8,128)(2,1)}) %reduce-scatter.33.cloned.1.call-update) | async-done | bytes 335888
  2182.7 35.3 %reduce-scatter.31.cloned.1.call-done = bf16[128,256]{1,0:T(8,128)(2,1)} async-done(((bf16[1024,256]{1,0:T(8,128)(2,1)}), bf16[128,256]{1,0:T(8,128)(2,1)}) %reduce-scatter.31.cloned.1.call-update) | async-done | bytes 65552
  2219.7 40.6 %reduce-scatter.29.cloned.1.call-done = bf16[128,3,256]{2,0,1:T(8,128)(2,1)} async-done(((bf16[1024,3,256]{2,0,1:T(8,128)(2,1)}), bf16[128,3,256]{2,0,1:T(8,128)(2,1)}) %reduce-scatter.29.cloned.1.call-update) | async-done | bytes 196624 | tf_op jit(solution)/shard_map/reduce_scatter | solution.py:240
  2261.9 77.2 %reduce-scatter.27.cloned.1.call-done = bf16[512,1024]{1,0:T(8,128)(2,1)} async-done(((bf16[2048,1024]{1,0:T(8,128)(2,1)}), bf16[512,1024]{1,0:T(8,128)(2,1)}) %reduce-scatter.27.cloned.1.call-update) | async-done | bytes 1048592 | tf_op jit(solution)/shard_map/reduce_scatter | solution.py:229
  2343.9 40.9 %all-reduce.4 = (f32[1024]{0:T(1024)}, f32[1024]{0:T(1024)}) all-reduce(f32[1024]{0:T(1024)S(1)} %get-tuple-element.221, f32[1024]{0:T(1024)S(1)} %copy-done.34), channel_id=1, replica_groups=mesh['dp'=2,'ctx'=4,'tp'=4] {'dp','ctx','tp'}, use_global_device_ids=true, to_apply=%region_29.30 | all-reduce | flops 2048 | bytes 16384 | tf_op jit(solution)/shard_map/psum | solution.py:253
  (286 shorter events, 1037.9 us)
Async XLA Ops:
  7.2 825.1 %copy-start = (bf16[1024,2,656]{0,2,1:T(8,128)(2,1)S(1)}, bf16[1024,2,656]{0,2,1:T(8,128)(2,1)}, u32[]{:S(2)}) copy-start(bf16[1024,2,656]{0,2,1:T(8,128)(2,1)} %param.18) | copy-start | bytes 8060932
  7.2 91.4 %all-gather.8.cloned.1.call-start = ((), (), s32[]{:S(2)}) async-start(), calls=%async_computation.10 | async-start | bytes 5242880 | tf_op jit(solution)/shard_map/all_gather | solution.py:97
  15.0 128.0 %all-gather.10.cloned.1.call-start = ((), (), s32[]{:S(2)}) async-start(), calls=%async_computation.11 | async-start | bytes 5242880 | tf_op jit(solution)/shard_map/all_gather | solution.py:110
  109.8 69.8 %all-gather.18.cloned.1.call-start = ((), (), s32[]{:S(2)}) async-start(), calls=%async_computation.22 | async-start | bytes 5242880 | tf_op jit(solution)/shard_map/all_gather | solution.py:111
  112.6 555.5 %reduce-scatter.17.cloned.1.call-start = ((), (), s32[]{:S(2)}) async-start(), calls=%async_computation.12 | async-start | bytes 10485760 | tf_op jit(solution)/shard_map/reduce_scatter | solution.py:136
  523.4 228.1 %all-gather.14.cloned.1.call-start = ((), (), s32[]{:S(2)}) async-start(), calls=%async_computation.15 | async-start | bytes 5242880 | tf_op jit(solution)/shard_map/all_gather | solution.py:157
  524.1 501.7 %copy-start.35 = (pred[512]{0:T(512)(128)(4,1)}, pred[512]{0:T(512)(128)(4,1)S(1)}, u32[]{:S(2)}) copy-start(pred[512]{0:T(512)(128)(4,1)S(1)} %add_compare_fusion) | copy-start | bytes 1540
  526.5 305.8 %all-gather.12.cloned.1.call-start = ((), (), s32[]{:S(2)}) async-start(), calls=%async_computation.13 | async-start | bytes 5242880 | tf_op jit(solution)/shard_map/all_gather | solution.py:143
  672.8 270.1 %reduce-scatter.21.cloned.1.call-start = ((), (), s32[]{:S(2)}) async-start(), calls=%async_computation.16 | async-start | bytes 5242880 | tf_op jit(solution)/shard_map/reduce_scatter | solution.py:165
  867.5 155.2 %reduce-scatter.19.cloned.1.call-start = ((), (), s32[]{:S(2)}) async-start(), calls=%async_computation.14 | async-start | bytes 5242880 | tf_op jit(solution)/shard_map/reduce_scatter | solution.py:149
  875.7 235.6 %all-gather.16.cloned.1.call-start = ((), (), s32[]{:S(2)}) async-start(), calls=%async_computation.17 | async-start | bytes 5242880 | tf_op jit(solution)/shard_map/all_gather | solution.py:175
  1029.9 1015.3 %reduce-scatter.23.cloned.1.call-start = ((), (), s32[]{:S(2)}) async-start(), calls=%async_computation.18 | async-start | bytes 5242880 | tf_op jit(solution)/shard_map/reduce_scatter | solution.py:219
  2000.2 90.5 %reduce-scatter.25.cloned.1.call-start = ((), (), s32[]{:S(2)}) async-start(), calls=%async_computation.19 | async-start | bytes 5242880 | tf_op jit(solution)/shard_map/reduce_scatter | solution.py:222
  2012.8 119.6 %reduce-scatter.35.cloned.1.call-start = ((), (), s32[]{:S(2)}) async-start(), calls=%async_computation.25 | async-start | bytes 1769472
  2023.4 157.2 %reduce-scatter.33.cloned.1.call-start = ((), (), s32[]{:S(2)}) async-start(), calls=%async_computation.24 | async-start | bytes 3244032
  2037.7 180.3 %reduce-scatter.31.cloned.1.call-start = ((), (), s32[]{:S(2)}) async-start(), calls=%async_computation.23 | async-start | bytes 589824
  2045.1 215.1 %reduce-scatter.29.cloned.1.call-start = ((), (), s32[]{:S(2)}) async-start(), calls=%async_computation.21 | async-start | bytes 1769472 | tf_op jit(solution)/shard_map/reduce_scatter | solution.py:240
  2098.2 240.9 %reduce-scatter.27.cloned.1.call-start = ((), (), s32[]{:S(2)}) async-start(), calls=%async_computation.20 | async-start | bytes 5242880 | tf_op jit(solution)/shard_map/reduce_scatter | solution.py:229
  2105.6 233.6 %copy-start.27 = (f32[512]{0:T(512)S(1)}, f32[512]{0:T(512)}, u32[]{:S(2)}) copy-start(f32[512]{0:T(512)} %copy-done.26) | copy-start | bytes 6148
  2105.6 235.4 %copy-start.33 = (f32[512]{0:T(512)S(1)}, f32[512]{0:T(512)}, u32[]{:S(2)}) copy-start(f32[512]{0:T(512)} %copy-done.32) | copy-start | bytes 6148
  2105.6 235.4 %copy-start.29 = (f32[512]{0:T(512)S(1)}, f32[512]{0:T(512)}, u32[]{:S(2)}) copy-start(f32[512]{0:T(512)} %copy-done.28) | copy-start | bytes 6148
  2105.6 238.2 %copy-start.34 = (f32[1024]{0:T(1024)S(1)}, f32[1024]{0:T(1024)}, u32[]{:S(2)}) copy-start(f32[1024]{0:T(1024)} %get-tuple-element.219) | copy-start | bytes 12292
  2105.6 279.1 %copy-start.31 = (f32[512]{0:T(512)S(1)}, f32[512]{0:T(512)}, u32[]{:S(2)}) copy-start(f32[512]{0:T(512)} %copy-done.30) | copy-start | bytes 6148
  2105.6 279.1 %copy-start.36 = (pred[512]{0:T(512)(128)(4,1)S(1)}, pred[512]{0:T(512)(128)(4,1)}, u32[]{:S(2)}) copy-start(pred[512]{0:T(512)(128)(4,1)} %copy-done.35) | copy-start | bytes 1540
  (43 other events, 1431.5 us)
Sparse Core Ops, SparseCore 0:
  15.1 83.4 all-gather.7
  109.9 33.0 all-gather.9
  145.1 34.4 all-gather.17
  523.5 144.4 reduce-scatter.16
  670.0 81.4 all-gather.13
  753.0 79.2 all-gather.11
  867.6 75.2 reduce-scatter.20
  945.3 77.2 reduce-scatter.18
  1030.0 81.2 all-gather.15
  2000.3 43.0 reduce-scatter.22
  2046.1 44.5 reduce-scatter.24
  2093.8 38.4 reduce-scatter.34
  2135.7 44.8 reduce-scatter.32
  2183.9 34.1 reduce-scatter.30
  2221.7 38.4 reduce-scatter.28
  2262.4 76.7 reduce-scatter.26
where the time goes:
time: 2400 us
  waiting for transfers between devices  931 us (39%)
  matrix products  893 us (37%)
  other arithmetic  419 us (17%)
  local copies, waits for them, and re-layouts  94.4 us (4%)
  blocking collectives  40.9 us (2%)
    convert_element_type x4, other arithmetic, query_side(): d_scores = (probs * (d_probs - row_delta[:, :, None])).astype(jnp.bfloat16)  217 us
    dot_general x4, matrix products, query_side(): jnp.einsum('qhd,khd->hqk', grad_block, value_heads, preferred_element_typ...  207 us
    reduce_scatter x1, waiting for transfers between devices, body(): lax.psum_scatter(jnp.dot(attended, out_weight, preferred_element_type=jnp...  141 us
    dot_general x4, matrix products, query_side(): jnp.einsum('hqk,qhd->khd', probs.astype(jnp.bfloat16), grad_block, prefer...  123 us
    dot_general x4, matrix products, forward_block(): jnp.einsum('qhd,khd->hqk', query_block, key_heads, preferred_element_type...  113 us
    dot_general x4, matrix products, forward_block(): jnp.einsum('hqk,khd->qhd', weights, value_heads, preferred_element_type=j...  109 us
    unnamed x19, waiting for transfers between devices  109 us
    dot_general x4, matrix products, recompute(): jnp.einsum('qhd,khd->hqk', query_block, key_part, preferred_element_type=...  104 us
  transfers between devices with their start and end apart: 16, of which 15 were waited for; matrix products, arithmetic and copies ran while one was open for 4% of the time, Pallas kernels for 0%

commit v1 on v0

v1 whole, which is shorter than its diff:
```python
from functools import partial
import math

import jax
import jax.numpy as jnp
from jax import lax
from jax.experimental import pallas as pl
from jax.experimental.pallas import tpu as pltpu
from jax.sharding import PartitionSpec as P

HD = 64
HALF = HD // 2
EPS = 1e-05
THETA = 160000.0
NEG = -1e30
LOG2E = 1.4426950408889634
LN2 = 0.6931471805599453
BF = jnp.bfloat16
F32 = jnp.float32
ROWS_V = HD + 16


def dot(a, b, dims):
    return lax.dot_general(a, b, (dims, ((), ())), preferred_element_type=F32)


def layout(length_row, row_length):
    count = length_row.shape[0]
    order = lax.iota(jnp.int32, count)
    ends = jnp.sum(jnp.where(order[:, None] <= order[None, :], length_row[:, None], 0), axis=0)
    places = lax.iota(jnp.int32, row_length)
    passed = places[:, None] >= ends[None, :]
    start = jnp.max(jnp.where(passed, ends[None, :], 0), axis=1)
    end = jnp.min(jnp.where(passed, row_length, ends[None, :]), axis=1)
    return start, end, ends[count - 1]


def ranges(q_start, q_end, rows, keys):
    first = q_start.reshape(-1, rows)[:, 0]
    last = q_end.reshape(-1, rows)[:, -1]
    first_end = q_end.reshape(-1, rows)[:, 0]
    lo = first // keys
    hi = (last + keys - 1) // keys
    flo = (first + keys - 1) // keys
    fhi = last // keys
    plain = (first_end == last) & (fhi > flo)
    return jnp.stack([lo, hi, jnp.where(plain, flo, hi), jnp.where(plain, fhi, hi)])


def normalize(values, gain):
    mean = jnp.mean(values, axis=-1, keepdims=True)
    centered = values - mean
    inverse = lax.rsqrt(jnp.mean(centered * centered, axis=-1, keepdims=True) + EPS)
    return centered * inverse * gain, centered, inverse


def normalize_back(grad, centered, inverse, gain):
    scaled = grad * gain
    shift = jnp.mean(scaled, axis=-1, keepdims=True)
    along = jnp.mean(scaled * centered, axis=-1, keepdims=True)
    back = inverse * (scaled - shift) - centered * (inverse * inverse * inverse * along)
    return back, jnp.sum(grad * centered * inverse, axis=0)


def allowed(block, keys, start, end):
    at = block * keys + lax.broadcasted_iota(jnp.int32, (keys, 1), 0)
    return (at >= start) & (at < end)


def prepare(source, target):
    chunk = source.shape[-1]
    for c in range(source.shape[0]):
        target[pl.ds(c * chunk, chunk), :] = source[c, 0, 0].astype(F32).T.astype(BF)


def forward_kernel(keys, table, start_ref, end_ref, q_ref, k_ref, v_ref, o_ref, lse_ref, k_rows, v_cols):
    i = pl.program_id(1)
    chunk = k_ref.shape[-1]

    @pl.when(i == 0)
    def _():
        prepare(k_ref, k_rows)
        for c in range(k_ref.shape[0]):
            at = pl.ds(c * chunk, chunk)
            v_cols[:HD, at] = v_ref[c, 0, 0]
            ones = lax.broadcasted_iota(jnp.int32, (ROWS_V - HD, chunk), 0) == 0
            v_cols[HD:, at] = jnp.where(ones, 1.0, 0.0).astype(BF)

    q = q_ref[0, 0, 0]
    rows = q.shape[1]
    start, end = start_ref[...], end_ref[...]

    def step(masked, block, carry):
        peak, total = carry
        at = pl.multiple_of(block * keys, keys)
        scores = dot(k_rows[pl.ds(at, keys), :], q, ((1,), (0,)))
        if masked:
            scores = jnp.where(allowed(block, keys, start, end), scores, NEG)
        new_peak = jnp.maximum(peak, jnp.max(scores, axis=0, keepdims=True))
        weights = jnp.exp2(scores - new_peak).astype(BF)
        total = total * jnp.exp2(peak - new_peak) + dot(v_cols[:, pl.ds(at, keys)], weights, ((1,), (0,)))
        return new_peak, total

    carry = (jnp.full((1, rows), NEG, F32), jnp.zeros((ROWS_V, rows), F32))
    lo, hi, flo, fhi = (table[j, i] for j in range(4))
    carry = lax.fori_loop(lo, flo, partial(step, True), carry)
    carry = lax.fori_loop(flo, fhi, partial(step, False), carry)
    peak, total = lax.fori_loop(fhi, hi, partial(step, True), carry)
    weight = total[HD : HD + 1]
    o_ref[0, 0] = (total[:HD] / weight).astype(BF)
    lse_ref[0] = peak + jnp.log2(weight)


def attend(table, start, end, q, k, v, share, rows, keys):
    (q, qj), (k, kj), (v, vj) = q, k, v
    q_chunks, _, heads, _, chunk = q.shape
    k_chunks = k.shape[0]
    tokens = q_chunks * chunk
    per_chunk, per_share = chunk // rows, share // rows
    row_spec = pl.BlockSpec((1, rows), lambda h, i, t: (0, i))
    whole = (k_chunks, 1, 1, HD, chunk)
    return pl.pallas_call(
        partial(forward_kernel, keys),
        out_shape=(
            jax.ShapeDtypeStruct((tokens // share, heads, HD, share), BF),
            jax.ShapeDtypeStruct((heads, 1, tokens), F32),
        ),
        grid_spec=pltpu.PrefetchScalarGridSpec(
            num_scalar_prefetch=1,
            grid=(heads, tokens // rows),
            in_specs=[
                row_spec,
                row_spec,
                pl.BlockSpec((1, 1, 1, HD, rows), lambda h, i, t: (i // per_chunk, qj, h, 0, i % per_chunk)),
                pl.BlockSpec(whole, lambda h, i, t: (0, kj, h, 0, 0)),
                pl.BlockSpec(whole, lambda h, i, t: (0, vj, h, 0, 0)),
            ],
            out_specs=[
                pl.BlockSpec((1, 1, HD, rows), lambda h, i, t: (i // per_share, h, 0, i % per_share)),
                pl.BlockSpec((1, 1, rows), lambda h, i, t: (h, 0, i)),
            ],
            scratch_shapes=[
                pltpu.VMEM((k_chunks * chunk, HD), BF),
                pltpu.VMEM((ROWS_V, k_chunks * chunk), BF),
            ],
        ),
        compiler_params=pltpu.CompilerParams(vmem_limit_bytes=48 << 20),
        name="attend",
    )(table, start, end, q, k, v)


def backward_kernel(
    keys, scale, table, start_ref, end_ref, lse_ref, q_ref, k_ref, v_ref, o_ref, g_ref, dq_ref, dkv_ref,
    k_rows, v_rows, dk_sum, dv_sum,
):
    i = pl.program_id(1)
    chunk = k_ref.shape[-1]
    per_chunk = chunk // keys

    @pl.when(i == 0)
    def _():
        prepare(k_ref, k_rows)
        prepare(v_ref, v_rows)
        dk_sum[...] = jnp.zeros_like(dk_sum)
        dv_sum[...] = jnp.zeros_like(dv_sum)

    q, g = q_ref[0, 0, 0], g_ref[0, 0]
    rows = q.shape[1]
    q_rows, g_rows = q.astype(F32).T.astype(BF), g.astype(F32).T.astype(BF)
    delta = jnp.sum(g.astype(F32) * o_ref[0, 0].astype(F32), axis=0, keepdims=True)
    lse = lse_ref[0]
    start, end = start_ref[...], end_ref[...]

    def step(masked, block, dq):
        at = pl.multiple_of(block * keys, keys)
        here = pl.ds(at, keys)
        probs = jnp.exp2(dot(k_rows[here, :], q, ((1,), (0,))) - lse)
        if masked:
            probs = jnp.where(allowed(block, keys, start, end), probs, 0.0)
        d_probs = dot(v_rows[here, :], g, ((1,), (0,)))
        d_scores = (probs * (d_probs - delta)).astype(BF)
        dv_sum[here, :] += dot(probs.astype(BF), g_rows, ((1,), (0,)))
        dk_sum[here, :] += dot(d_scores, q_rows, ((1,), (0,)))
        columns = pl.ds(pl.multiple_of((block % per_chunk) * keys, keys), keys)
        return dq + dot(k_ref[block // per_chunk, 0, 0, :, columns], d_scores, ((1,), (0,)))

    lo, hi, flo, fhi = (table[j, i] for j in range(4))
    dq = jnp.zeros((HD, rows), F32)
    dq = lax.fori_loop(lo, flo, partial(step, True), dq)
    dq = lax.fori_loop(flo, fhi, partial(step, False), dq)
    dq = lax.fori_loop(fhi, hi, partial(step, True), dq)
    dq_ref[0, 0] = (dq * scale).astype(BF)

    @pl.when(i == pl.num_programs(1) - 1)
    def _():
        for c in range(k_ref.shape[0]):
            at = pl.ds(c * chunk, chunk)
            dkv_ref[c, 0, 0] = (dk_sum[at, :].T * LN2).astype(BF)
            dkv_ref[c, 1, 0] = dv_sum[at, :].T.astype(BF)


def attend_back(table, start, end, lse, q, k, v, out, grad, share, rows, keys, scale):
    (q, qj), (k, kj), (v, vj) = q, k, v
    q_chunks, _, heads, _, chunk = q.shape
    k_chunks = k.shape[0]
    tokens = q_chunks * chunk
    per_chunk, per_share = chunk // rows, share // rows
    row_spec = pl.BlockSpec((1, rows), lambda h, i, t: (0, i))
    whole = (k_chunks, 1, 1, HD, chunk)
    share_spec = pl.BlockSpec((1, 1, HD, rows), lambda h, i, t: (i // per_share, h, 0, i % per_share))
    return pl.pallas_call(
        partial(backward_kernel, keys, scale),
        out_shape=(
            jax.ShapeDtypeStruct((q_chunks, heads, HD, chunk), BF),
            jax.ShapeDtypeStruct((k_chunks, 2, heads, HD, chunk), BF),
        ),
        grid_spec=pltpu.PrefetchScalarGridSpec(
            num_scalar_prefetch=1,
            grid=(heads, tokens // rows),
            in_specs=[
                row_spec,
                row_spec,
                pl.BlockSpec((1, 1, rows), lambda h, i, t: (h, 0, i)),
                pl.BlockSpec((1, 1, 1, HD, rows), lambda h, i, t: (i // per_chunk, qj, h, 0, i % per_chunk)),
                pl.BlockSpec(whole, lambda h, i, t: (0, kj, h, 0, 0)),
                pl.BlockSpec(whole, lambda h, i, t: (0, vj, h, 0, 0)),
                share_spec,
                share_spec,
            ],
            out_specs=[
                pl.BlockSpec((1, 1, HD, rows), lambda h, i, t: (i // per_chunk, h, 0, i % per_chunk)),
                pl.BlockSpec((k_chunks, 2, 1, HD, chunk), lambda h, i, t: (0, 0, h, 0, 0)),
            ],
            scratch_shapes=[
                pltpu.VMEM((k_chunks * chunk, HD), BF),
                pltpu.VMEM((k_chunks * chunk, HD), BF),
                pltpu.VMEM((k_chunks * chunk, HD), F32),
                pltpu.VMEM((k_chunks * chunk, HD), F32),
            ],
        ),
        compiler_params=pltpu.CompilerParams(vmem_limit_bytes=56 << 20),
        name="attend_back",
    )(table, start, end, lse, q, k, v, out, grad)


def turn(pairs, cosine, sine):
    a, b = pairs[..., 0, :, :], pairs[..., 1, :, :]
    return jnp.stack([a * cosine - b * sine, b * cosine + a * sine], axis=-3)


def gelu_parts(gate):
    lower = 0.5 * (1.0 + lax.erf(gate * math.sqrt(0.5)))
    slope = lower + gate * (jnp.exp(-0.5 * gate * gate) * (1.0 / math.sqrt(2.0 * math.pi)))
    return gate * lower, slope


def body(hidden_in, attn_gain, qkv_weight, out_weight, mlp_gain, wide_weight, down_weight, lengths, cotangent):
    share, width = hidden_in.shape[1:]
    ctx, tp = lax.axis_size("ctx"), lax.axis_size("tp")
    copies = lax.axis_size("dp") * ctx
    group = share * tp
    length = group * ctx
    heads = qkv_weight.shape[2] // HD
    units = down_weight.shape[0]
    part = width // copies
    scale = 1.0 / math.sqrt(HD)
    copy_at = lax.axis_index("dp") * ctx + lax.axis_index("ctx")
    everywhere, reduced = ("tp", "dp", "ctx"), ("dp", "ctx")

    def rows_of(array, dim):
        size = array.shape[dim] // copies
        return lax.dynamic_slice_in_dim(array, copy_at * size, size, dim)

    def gather(array):
        return lax.all_gather(array, everywhere, axis=0, tiled=True)

    start, end, filled_to = layout(lengths[0], length)
    group_at = lax.axis_index("ctx") * group
    share_at = group_at + lax.axis_index("tp") * share
    live = (share_at + lax.iota(jnp.int32, share) < filled_to)[:, None]
    places = group_at + lax.iota(jnp.int32, group)
    in_doc = places - lax.dynamic_slice_in_dim(start, group_at, group)
    frequency = jnp.exp(lax.iota(F32, HALF) * (-2.0 * math.log(THETA) / HD))
    angles = frequency[:, None] * in_doc.astype(F32)[None, :]
    cosine, sine = jnp.cos(angles), jnp.sin(angles)

    inputs = hidden_in[0].astype(F32)
    gain_one, gain_two = attn_gain.astype(F32), mlp_gain.astype(F32)
    normed, centered, inverse = normalize(inputs, gain_one)
    normed_full = lax.all_gather(normed.astype(BF), "tp", axis=0, tiled=True)

    out_full = gather(rows_of(out_weight, 0))
    wide_full = gather(rows_of(wide_weight, 0).reshape(part, 2 * units)).reshape(tp, width, 2 * units)
    down_full = gather(rows_of(down_weight, 1).T).reshape(tp, width, units)

    mixed = dot(qkv_weight.reshape(width, 3 * heads * HD), normed_full, ((0,), (1,)))
    mixed = mixed.reshape(3, heads, 2, HALF, group)
    mixed = jnp.stack(
        [
            turn(mixed[0], cosine, sine) * (scale * LOG2E),
            turn(mixed[1], cosine, sine),
            mixed[2],
        ]
    ).astype(BF)

    spread = heads % ctx == 0
    rows = min(512, share)
    if spread:
        own = heads // ctx
        mixed = mixed.reshape(3, ctx, own, HD, group).transpose(1, 0, 2, 3, 4)
        mixed = lax.all_to_all(mixed, "ctx", 0, 0, tiled=True)
        queries, key_side, value_side = (mixed, 0), (mixed, 1), (mixed, 2)
        q_start, q_end = start, end
    else:
        mixed = mixed.reshape(3, heads, HD, group)
        both = lax.all_gather(mixed[1:], "ctx", axis=0)
        queries, key_side, value_side = (mixed[:1][None], 0), (both, 0), (both, 1)
        q_start = lax.dynamic_slice_in_dim(start, group_at, group)
        q_end = lax.dynamic_slice_in_dim(end, group_at, group)
    keys = 512
    table = ranges(q_start, q_end, rows, keys)
    q_start, q_end = q_start[None], q_end[None]
    shares, lse = attend(table, q_start, q_end, queries, key_side, value_side, share, rows, keys)
    if spread:
        attended = lax.all_to_all(shares, ("ctx", "tp"), 0, 0, tiled=True)
        attended = attended.reshape(ctx, tp, own * HD, share).transpose(1, 0, 2, 3)
    else:
        attended = lax.all_to_all(shares, "tp", 0, 0, tiled=True)
    attended = attended.reshape(width, share)

    middle = inputs + dot(attended, out_full, ((0,), (0,)))
    normed_two, centered_two, inverse_two = normalize(middle, gain_two)
    normed_two = normed_two.astype(BF)
    grad = jnp.where(live, cotangent[0], jnp.zeros_like(cotangent[0]))
    mlp_out = jnp.zeros((share, width), F32)
    d_normed_two = jnp.zeros((share, width), F32)
    products, d_wides = [], []
    for s in range(tp):
        wide = dot(normed_two, wide_full[s], ((1,), (0,)))
        up = wide[:, units:]
        active, slope = gelu_parts(wide[:, :units])
        product = (active * up).astype(BF)
        d_product = dot(grad, down_full[s], ((1,), (0,)))
        d_wide = jnp.concatenate([d_product * up * slope, d_product * active], axis=1).astype(BF)
        mlp_out = mlp_out + dot(product, down_full[s], ((1,), (1,)))
        d_normed_two = d_normed_two + dot(d_wide, wide_full[s], ((1,), (1,)))
        products.append(product)
        d_wides.append(d_wide)
    product, d_wide = jnp.concatenate(products, axis=1), jnp.concatenate(d_wides, axis=1)
    result = jnp.where(live, middle + mlp_out, 0.0).astype(BF)
    back_two, gain_two_grad = normalize_back(d_normed_two, centered_two, inverse_two, gain_two)
    d_middle = grad.astype(F32) + back_two
    d_branch = d_middle.astype(BF)
    d_attended = dot(out_full, d_branch, ((1,), (1,))).astype(BF)

    wide_grad = dot(normed_two, d_wide, ((0,), (0,))).astype(BF)
    down_grad = dot(grad, product, ((0,), (0,))).astype(BF)
    out_grad = dot(d_branch, attended, ((0,), (1,))).astype(BF)

    def reduce(partial_sum):
        mine = lax.psum_scatter(partial_sum, reduced, scatter_dimension=0, tiled=True)
        mine = mine.reshape(part, tp, -1).transpose(1, 0, 2)
        return lax.psum_scatter(mine, "tp", scatter_dimension=0, tiled=False).astype(F32)

    wide_part = reduce(wide_grad).reshape(part, 2, units)
    down_part = reduce(down_grad).T
    out_part = reduce(out_grad).T

    if spread:
        d_shares = d_attended.reshape(tp, ctx, own * HD, share).transpose(1, 0, 2, 3)
        d_shares = d_shares.reshape(tp * ctx, own, HD, share)
        d_shares = lax.all_to_all(d_shares, ("ctx", "tp"), 0, 0, tiled=True)
    else:
        d_shares = lax.all_to_all(d_attended.reshape(tp, heads, HD, share), "tp", 0, 0, tiled=True)
    dq, dkv = attend_back(
        table, q_start, q_end, lse, queries, key_side, value_side, shares, d_shares, share, rows, keys, scale
    )
    if spread:
        d_mixed = jnp.concatenate([dq[:, None], dkv], axis=1)
        d_mixed = lax.all_to_all(d_mixed, "ctx", 0, 0, tiled=True)
        d_mixed = d_mixed.transpose(1, 0, 2, 3, 4)
    else:
        dkv = lax.psum_scatter(dkv, "ctx", scatter_dimension=0, tiled=False)
        d_mixed = jnp.concatenate([dq, dkv], axis=0)
    d_mixed = d_mixed.reshape(3, heads, 2, HALF, group).astype(F32)
    d_mixed = jnp.stack([turn(d_mixed[0], cosine, -sine), turn(d_mixed[1], cosine, -sine), d_mixed[2]])
    d_mixed = d_mixed.astype(BF).reshape(3 * heads * HD, group)
    qkv_grad = dot(normed_full, d_mixed, ((0,), (1,))).astype(BF)
    d_normed = dot(d_mixed, qkv_weight.reshape(width, 3 * heads * HD), ((0,), (1,))).astype(BF)
    d_normed = lax.psum_scatter(d_normed, "tp", scatter_dimension=0, tiled=True).astype(F32)
    qkv_part = lax.psum_scatter(qkv_grad, reduced, scatter_dimension=0, tiled=True).astype(F32)
    qkv_part = qkv_part.reshape(part, 3, heads * HD)
    back_one, gain_one_grad = normalize_back(d_normed, centered, inverse, gain_one)
    input_grad = d_middle + back_one
    gain_one_sum, gain_two_sum = lax.psum((gain_one_grad, gain_two_grad), ("dp", "ctx", "tp"))
    return (
        result[None],
        input_grad[None],
        qkv_part,
        out_part,
        wide_part,
        down_part,
        gain_one_sum,
        gain_two_sum,
    )


def solution(mesh):
    tokens = P("dp", ("ctx", "tp"), None)
    placed = (tokens, P(), P(None, None, "tp"), P("tp", None), P(), P(None, None, "tp"), P("tp", None), P("dp", None), tokens)
    return jax.shard_map(
        body,
        mesh=mesh,
        in_specs=placed,
        out_specs=(
            tokens,
            tokens,
            P(("dp", "ctx"), None, "tp"),
            P("tp", ("dp", "ctx")),
            P(("dp", "ctx"), None, "tp"),
            P("tp", ("dp", "ctx")),
            P(),
            P(),
        ),
        check_vma=False,
    )
```

time: 2400 us -> 843 us (0.35)
  matrix products: 893 us -> 88.8 us
  waiting for transfers between devices: 931 us -> 363 us
  other arithmetic: 419 us -> 37.8 us
  Pallas kernels: 0 us -> 202 us
  local copies, waits for them, and re-layouts: 94.4 us -> 40.1 us
  blocking collectives: 40.9 us -> 73.3 us
    dot_general x40 -> x24, matrix products: 893 us -> 88.8 us  [dot(): return lax.dot_general(a, b, (dims, ((), ())), preferred_element_type=F32)]
    reduce_scatter x7, waiting for transfers between devices: 444 us -> 107 us  [the longest x1 76.4 us: body(): lax.psum_scatter(d_normed, 'tp', scatter_dimension=0, tiled=True)]
    all_gather x6 -> x4, waiting for transfers between devices: 378 us -> 139 us  [the longest x1 75.4 us: body(): normed_full = lax.all_gather(normed.astype(BF), 'tp', axis=0, tiled=True)]
    convert_element_type x16 -> x12, other arithmetic: 241 us -> 11.1 us  [the longest x4 3.46 us: body(): product = (active * up).astype(BF)]
    pallas_call x0 -> x2, Pallas kernels: none -> 202 us  [the longest x1 116 us: attend_back(): pl.pallas_call(partial(backward_kernel, keys, scale), out_shape=(jax.Shap...]
    all_to_all x0 -> x3, waiting for transfers between devices: none -> 117 us  [the longest x1 41.3 us: body(): mixed = lax.all_to_all(mixed, 'ctx', 0, 0, tiled=True)]
    unnamed x19 -> x13, waiting for transfers between devices: 109 us -> 0.21 us
    reduce_sum x14 -> x5, other arithmetic: 107 us -> 5.96 us  [the longest x1 2.29 us: normalize_back(): return (back, jnp.sum(grad * centered * inverse, axis=0))]
  transfers between devices with their start and end apart: 16 -> 15, of which waited for: 15 -> 8; matrix products, arithmetic and copies ran while one was open for 4% -> 14% of each run, Pallas kernels for 0% -> 24%
where the time goes in v1:
time: 843 us; the launch traced here: 834 us
  waiting for transfers between devices  363 us (43%)
  Pallas kernels  202 us (24%)
  matrix products  88.8 us (11%)
  blocking collectives  73.3 us (9%)
  local copies, waits for them, and re-layouts  40.1 us (5%)
  other arithmetic  37.8 us (4%)
  between operations  15.5 us (2%)
  starting transfers between devices  13.3 us (2%)
    pallas_call x1, Pallas kernels, attend_back(): pl.pallas_call(partial(backward_kernel, keys, scale), out_shape=(jax.Shap...  116 us
    dot_general x24, matrix products, dot(): return lax.dot_general(a, b, (dims, ((), ())), preferred_element_type=F32)  88.8 us
    pallas_call x1, Pallas kernels, attend(): pl.pallas_call(partial(forward_kernel, keys), out_shape=(jax.ShapeDtypeSt...  86 us
    reduce_scatter x1, waiting for transfers between devices, body(): lax.psum_scatter(d_normed, 'tp', scatter_dimension=0, tiled=True)  76.4 us
    all_gather x1, waiting for transfers between devices, body(): normed_full = lax.all_gather(normed.astype(BF), 'tp', axis=0, tiled=True)  75.4 us
    all_gather x3, waiting for transfers between devices, gather(): return lax.all_gather(array, everywhere, axis=0, tiled=True)  63.2 us
    psum x1, blocking collectives, body(): lax.psum((gain_one_grad, gain_two_grad), ('dp', 'ctx', 'tp'))  42.7 us
    all_to_all x1, waiting for transfers between devices, body(): mixed = lax.all_to_all(mixed, 'ctx', 0, 0, tiled=True)  41.3 us
  transfers between devices with their start and end apart: 15, of which 8 were waited for; matrix products, arithmetic and copies ran while one was open for 14% of the time, Pallas kernels for 24%

profile of v1, /device:TPU:0, one launch (start us, length us, event | category | flops | bytes accessed | tf_op | source)
XLA Modules:
  0.0 834.2 jit_solution(16612426645030460800)
XLA Ops:
  20.1 75.4 %all-gather.5.cloned.1.call-done = bf16[2048,1024]{1,0:T(8,128)(2,1)} async-done(((bf16[512,1024]{1,0:T(8,128)(2,1)}), bf16[2048,1024]{1,0:T(8,128)(2,1)}) %all-gather.5.cloned.1.call-update) | async-done | bytes 4194320 | tf_op jit(solution)/shard_map/all_gather | solution.py:290
  95.5 5.3 convolution_bitcast_fusion
  108.6 41.3 %all-to-all-done.q_ref.k_ref.v_ref = bf16[4,3,1,64,2048]{4,3,2,1,0:T(8,128)(2,1)S(1)} async-done(((bf16[4,3,1,64,2048]{4,3,2,1,0:T(8,128)(2,1)}), bf16[4,3,1,64,2048]{4,3,2,1,0:T(8,128)(2,1)S(1)}, u32[]{:S(2)}, u32[]{:S(2)}) %all-to-all-start) | async-done | bytes 3145760 | tf_op jit(solution)/shard_map/all_to_all | solution.py:311
  149.9 86.0 %attend.1 = (bf16[16,1,64,512]{3,2,1,0:T(8,128)(2,1)S(1)}, f32[1,1,8192]{2,1,0:T(1,128)S(1)}) custom-call(s32[4,16]{1,0:T(4,128)S(1)} %pad_add_fusion.table, s32[1,8192]{1,0:T(1,128)S(1)} %bitcast.221, s32[1,8192]{1,0:T(1,128)S(1)} %bitcast.223, bf16[4,3,1,64,2048]{4,3,2,1,0:T(8,128)(2,1)S(1)} %all-to-all-done.q_ref.k_ref.v_ref, ...), custom_call_target="tpu_custom_call" | custom-call | tf_op jit(solution)/shard_map/attend/pallas_call | solution.py:122
  242.8 41.0 %all-to-all-done.1 = bf16[16,1,64,512]{3,2,1,0:T(8,128)(2,1)S(1)} async-done(((bf16[16,1,64,512]{3,2,1,0:T(8,128)(2,1)}), bf16[16,1,64,512]{3,2,1,0:T(8,128)(2,1)S(1)}, u32[]{:S(2)}, u32[]{:S(2)}) %all-to-all-start.1) | async-done | bytes 1048608 | tf_op jit(solution)/shard_map/all_to_all | solution.py:325
  289.9 5.3 fusion.29
  295.2 63.2 %all-gather.11.cloned.1.call-done = bf16[4096,656]{0,1:T(8,128)(2,1)} async-done(((bf16[128,656]{0,1:T(8,128)(2,1)}), bf16[4096,656]{0,1:T(8,128)(2,1)}) %all-gather.11.cloned.1.call-update) | async-done | bytes 5373968 | tf_op jit(solution)/shard_map/all_gather | solution.py:275
  358.4 4.0 constant_dynamic-update-slice_fusion.7
  400.6 8.5 %convolution_convert_fusion.1 = bf16[1024,2624]{0,1:T(8,128)(2,1)} fusion(bf16[512,656]{0,1:T(8,128)(2,1)S(1)} %multiply_convert_fusion.5, bf16[512,656]{0,1:T(8,128)(2,1)S(1)} %multiply_convert_fusion.6, bf16[512,656]{0,1:T(8,128)(2,1)S(1)} %multiply_convert_fusion.7, bf16[512,656]{0,1:T(8,128)(2,1)S(1)} %multiply_convert_fusion.8, ...), kind=kOutput, calls=%fused_computation.3 | convolution fusion | flops 2765422592 | bytes 9110016 | tf_op jit(solution)/shard_map/dot_general | solution.py:24
  409.1 8.3 copy.90
  417.5 11.4 %convolution_convert_fusion = bf16[1024,5248]{1,0:T(8,128)(2,1)} fusion(bf16[512,1024]{1,0:T(8,128)(2,1)} %multiply_convert_fusion, bf16[512,5248]{0,1:T(8,128)(2,1)} %copy-done.38), kind=kOutput, calls=%fused_computation | convolution fusion | flops 5508300800 | bytes 17170432 | tf_op jit(solution)/shard_map/dot_general | solution.py:24
  432.5 30.6 %all_to_all.20.g_ref = bf16[16,1,64,512]{3,2,1,0:T(8,128)(2,1)} all-to-all(bf16[16,1,64,512]{3,2,1,0:T(8,128)(2,1)S(1)} %bitcast.232), channel_id=1, replica_groups=mesh['dp'=2,'ctx'=4,'tp'=4] {'ctx','tp'}, dimensions={0} | all-to-all | bytes 2097152 | tf_op jit(solution)/shard_map/all_to_all | solution.py:372
  463.1 115.9 %attend_back.1 = (bf16[4,1,64,2048]{3,2,1,0:T(8,128)(2,1)}, bf16[4,2,1,64,2048]{4,3,2,1,0:T(8,128)(2,1)}) custom-call(s32[4,16]{1,0:T(4,128)} %copy-done.7, s32[1,8192]{1,0:T(1,128)} %bitcast.222, s32[1,8192]{1,0:T(1,128)} %bitcast.224, f32[1,1,8192]{2,1,0:T(1,128)} %copy-done.6, bf16[4,3,1,64,2048]{4,3,2,1,0:T(8,128)(2,1)} %copy-done.2, ...), custom_call_target="tpu_custom_call" | custom-call | tf_op jit(solution)/shard_map/attend_back/pallas_call | solution.py:211
  579.0 3.8 pad_maximum_fusion
  582.9 4.7 all-to-all-start.3
  589.5 35.1 %all-to-all-done.3 = bf16[4,3,1,64,2048]{4,3,2,1,0:T(8,128)(2,1)} async-done(((bf16[4,3,1,64,2048]{4,3,2,1,0:T(8,128)(2,1)}), bf16[4,3,1,64,2048]{4,3,2,1,0:T(8,128)(2,1)}, u32[]{:S(2)}, u32[]{:S(2)}) %all-to-all-start.3) | async-done | bytes 3145760 | tf_op jit(solution)/shard_map/all_to_all | solution.py:380
  632.5 4.7 convolution_convert_fusion.4
  639.9 8.0 convolution_convert_fusion.2
  648.0 3.9 fusion.86
  664.8 8.2 reduce-scatter.13.cloned.1.call-done
  675.0 22.6 %reduce-scatter.23.cloned.1.call-done = bf16[1,128,656]{1,2,0:T(8,128)(2,1)} async-done(((bf16[4,128,656]{1,2,0:T(8,128)(2,1)}), bf16[1,128,656]{1,2,0:T(8,128)(2,1)}) %reduce-scatter.23.cloned.1.call-update) | async-done | bytes 167952 | tf_op jit(solution)/shard_map/reduce_scatter | solution.py:363
  699.2 76.4 %reduce-scatter.11.cloned.1.call-done = bf16[512,1024]{1,0:T(8,128)(2,1)} async-done(((bf16[2048,1024]{1,0:T(8,128)(2,1)}), bf16[512,1024]{1,0:T(8,128)(2,1)}) %reduce-scatter.11.cloned.1.call-update) | async-done | bytes 1048592 | tf_op jit(solution)/shard_map/reduce_scatter | solution.py:390
  778.0 42.7 %all-reduce = (f32[1024]{0:T(1024)}, f32[1024]{0:T(1024)}) all-reduce(f32[1024]{0:T(1024)S(1)} %get-tuple-element.59, f32[1024]{0:T(1024)S(1)} %get-tuple-element.56), channel_id=1, replica_groups=mesh['dp'=2,'ctx'=4,'tp'=4] {'dp','ctx','tp'}, use_global_device_ids=true, to_apply=%region_20.21 | all-reduce | flops 2048 | bytes 16384 | tf_op jit(solution)/shard_map/psum | solution.py:395
  820.7 4.3 fusion.36
  (209 shorter events, 108.3 us)
Async XLA Ops:
  7.2 88.3 %all-gather.5.cloned.1.call-start = ((), (), s32[]{:S(2)}) async-start(), calls=%async_computation.12 | async-start | bytes 5242880 | tf_op jit(solution)/shard_map/all_gather | solution.py:290
  11.9 273.0 %all-gather.7.cloned.1.call-start = ((), (), s32[]{:S(2)}) async-start(), calls=%async_computation.13 | async-start | bytes 2162688 | tf_op jit(solution)/shard_map/all_gather | solution.py:275
  13.5 276.4 %all-gather.9.cloned.1.call-start = ((), (), s32[]{:S(2)}) async-start(), calls=%async_computation.14 | async-start | bytes 11083776 | tf_op jit(solution)/shard_map/all_gather | solution.py:275
  14.4 344.0 %all-gather.11.cloned.1.call-start = ((), (), s32[]{:S(2)}) async-start(), calls=%async_computation.15 | async-start | bytes 5541888 | tf_op jit(solution)/shard_map/all_gather | solution.py:275
  17.8 83.0 %copy-start.23 = (bf16[1024,3,256]{0,2,1:T(8,128)(2,1)}, bf16[1024,3,256]{0,2,1:T(8,128)(2,1)S(1)}, u32[]{:S(2)}) copy-start(bf16[1024,3,256]{0,2,1:T(8,128)(2,1)S(1)} %copy.74) | copy-start | bytes 4718596
  17.9 82.9 %copy-start.36 = (s32[16]{0:T(128)}, s32[16]{0:T(128)S(1)}, u32[]{:S(2)}) copy-start(s32[16]{0:T(128)S(1)} %select_reduce_fusion.2) | copy-start | bytes 196
  18.3 131.6 %copy-start.4 = (s32[8192]{0:T(1024)}, s32[8192]{0:T(1024)S(1)}, u32[]{:S(2)}) copy-start(s32[8192]{0:T(1024)S(1)} %get-tuple-element.64) | copy-start | bytes 98308
  18.3 131.6 %copy-start.5 = (s32[8192]{0:T(1024)}, s32[8192]{0:T(1024)S(1)}, u32[]{:S(2)}) copy-start(s32[8192]{0:T(1024)S(1)} %get-tuple-element.65) | copy-start | bytes 98308
  104.6 45.3 %all-to-all-start = ((bf16[4,3,1,64,2048]{4,3,2,1,0:T(8,128)(2,1)}), bf16[4,3,1,64,2048]{4,3,2,1,0:T(8,128)(2,1)S(1)}, u32[]{:S(2)}, u32[]{:S(2)}) async-start(bf16[4,3,1,64,2048]{4,3,2,1,0:T(8,128)(2,1)} %maximum_bitcast_fusion), calls=%async_computation | async-start | bytes 6291456 | tf_op jit(solution)/shard_map/all_to_all | solution.py:311
  108.6 127.3 %copy-start.7 = (s32[4,16]{1,0:T(4,128)}, s32[4,16]{1,0:T(4,128)S(1)}, u32[]{:S(2)}) copy-start(s32[4,16]{1,0:T(4,128)S(1)} %pad_add_fusion.table) | copy-start | bytes 772
  149.9 86.1 %copy-start.2 = (bf16[4,3,1,64,2048]{4,3,2,1,0:T(8,128)(2,1)}, bf16[4,3,1,64,2048]{4,3,2,1,0:T(8,128)(2,1)S(1)}, u32[]{:S(2)}) copy-start(bf16[4,3,1,64,2048]{4,3,2,1,0:T(8,128)(2,1)S(1)} %all-to-all-done.q_ref.k_ref.v_ref) | copy-start | bytes 9437188
  237.5 47.4 %copy-start.9 = (bf16[1,512,1024]{2,1,0:T(8,128)(2,1)S(1)}, bf16[1,512,1024]{2,1,0:T(8,128)(2,1)}, u32[]{:S(2)}) copy-start(bf16[1,512,1024]{2,1,0:T(8,128)(2,1)} %param.9) | copy-start | bytes 3145732
  237.5 46.3 %all-to-all-start.1 = ((bf16[16,1,64,512]{3,2,1,0:T(8,128)(2,1)}), bf16[16,1,64,512]{3,2,1,0:T(8,128)(2,1)S(1)}, u32[]{:S(2)}, u32[]{:S(2)}) async-start(bf16[16,1,64,512]{3,2,1,0:T(8,128)(2,1)} %copy-done.3), calls=%async_computation.1 | async-start | bytes 2097152 | tf_op jit(solution)/shard_map/all_to_all | solution.py:325
  241.3 346.3 %reduce-scatter.15.cloned.1.call-start = ((), (), s32[]{:S(2)}) async-start(), calls=%async_computation.18 | async-start | bytes 2359296 | tf_op jit(solution)/shard_map/reduce_scatter | solution.py:361
  363.5 6.4 slice-start.3
  391.9 245.4 %reduce-scatter.25.cloned.1.call-start = ((), (), s32[]{:S(2)}) async-start(), calls=%async_computation.23 | async-start | bytes 6193152
  417.4 234.4 %reduce-scatter.19.cloned.1.call-start = ((), (), s32[]{:S(2)}) async-start(), calls=%async_computation.20 | async-start | bytes 12091392 | tf_op jit(solution)/shard_map/reduce_scatter | solution.py:361
  582.9 41.7 %all-to-all-start.3 = ((bf16[4,3,1,64,2048]{4,3,2,1,0:T(8,128)(2,1)}), bf16[4,3,1,64,2048]{4,3,2,1,0:T(8,128)(2,1)}, u32[]{:S(2)}, u32[]{:S(2)}) async-start(bf16[4,3,1,64,2048]{4,3,2,1,0:T(8,128)(2,1)} %pad_maximum_fusion), calls=%async_computation.3 | async-start | bytes 6291456 | tf_op jit(solution)/shard_map/all_to_all | solution.py:380
  587.5 75.8 %reduce-scatter.17.cloned.1.call-start = ((), (), s32[]{:S(2)}) async-start(), calls=%async_computation.19 | async-start | bytes 327680 | tf_op jit(solution)/shard_map/reduce_scatter | solution.py:363
  589.4 83.6 %reduce-scatter.13.cloned.1.call-start = ((), (), s32[]{:S(2)}) async-start(), calls=%async_computation.17 | async-start | bytes 1769472 | tf_op jit(solution)/shard_map/reduce_scatter | solution.py:391
  637.3 60.3 %reduce-scatter.23.cloned.1.call-start = ((), (), s32[]{:S(2)}) async-start(), calls=%async_computation.22 | async-start | bytes 839680 | tf_op jit(solution)/shard_map/reduce_scatter | solution.py:363
  639.6 136.1 %reduce-scatter.11.cloned.1.call-start = ((), (), s32[]{:S(2)}) async-start(), calls=%async_computation.16 | async-start | bytes 5242880 | tf_op jit(solution)/shard_map/reduce_scatter | solution.py:390
  647.9 177.1 %reduce-scatter.21.cloned.1.call-start = ((), (), s32[]{:S(2)}) async-start(), calls=%async_computation.21 | async-start | bytes 1679360 | tf_op jit(solution)/shard_map/reduce_scatter | solution.py:363
  663.3 157.4 %copy-start.33 = (f32[512]{0:T(512)S(1)}, f32[512]{0:T(512)}, u32[]{:S(2)}) copy-start(f32[512]{0:T(512)} %copy-done.32) | copy-start | bytes 6148
  (37 other events, 105.0 us)
Sparse Core Ops, SparseCore 0:
  12.0 83.4 all-gather.4
  99.0 57.4 all-gather.6
  159.8 123.9 all-gather.8
  287.1 71.1 all-gather.10
  392.1 39.3 reduce-scatter.14
  435.2 57.8 reduce-scatter.24
  496.6 82.8 reduce-scatter.18
  591.3 18.1 reduce-scatter.16
  637.4 35.5 reduce-scatter.12
  675.1 22.3 reduce-scatter.22
  700.0 75.6 reduce-scatter.10
  777.8 33.1 reduce-scatter.20
